TPU v7x, 32 devices: a whole 2x2x4 slice. The times are simulated.
32 devices in a mesh: grp: 2 (over y), seq: 8 (over z, x), mdl: 2 (over core).
Axes of the slice: x: 2, y: 2, z: 4, core: 2. Of those that a mesh axis runs over, the one named last changes fastest.
Arguments:
- signal: bfloat16 [2048, 2048], P(('grp', 'seq'), 'mdl'), parts along dimension 0, may hold values from -6 to 6
- gate_first: bfloat16 [2048, 2048], P(('grp', 'seq'), 'mdl'), parts along dimension 0, may hold values from -6 to 6
- gate_second: bfloat16 [2048, 2048], P(('grp', 'seq'), 'mdl'), parts along dimension 0, may hold values from -6 to 6
- spectrum_first: bfloat16 [2, 16, 128, 2048], P(None, 'seq', None, 'mdl'), may hold values from -8 to 8
- spectrum_second: bfloat16 [2, 16, 128, 2048], P(None, 'seq', None, 'mdl'), may hold values from -8 to 8
- skip_first: float32 [2048], P('mdl'), may hold values from 0.5 to 1.5
- skip_second: float32 [2048], P('mdl'), may hold values from 0.5 to 1.5
- out_weight: bfloat16 [2048, 2048], P('seq', 'mdl'), may hold values from -0.125 to 0.125
Outputs:
- block_out: bfloat16 [2048, 2048], P(('grp', 'seq'), 'mdl'), parts along dimension 0
There are 2 independent parts, one for each index of `grp`. A program takes and returns all parts, laid end to end along the dimension named above; an argument that names none is the same for every part. Nothing has to cross between parts.
All inputs are finite; a program needn't handle non-finite values.
Results may differ from a plain program's by a relative error of at most 0.0057.
Values may be sent and summed in bfloat16 or wider, within the bound.
A program may use at most 64 MiB of HBM per device.

v0:
```python
import math

import jax
import jax.numpy as jnp
from jax import lax
from jax.sharding import PartitionSpec as P


def angle_grid(first, second, modulus):
    product = first[:, None] * second[None, :] % modulus
    angles = product.astype(jnp.float32) * (2.0 * math.pi / modulus)
    return (jnp.cos(angles), jnp.sin(angles))


def mixing(form, left, right):
    return jnp.einsum(form, left, right, precision=lax.Precision.HIGHEST)


def complex_mix(form, real_table, imag_table, values_re, values_im):
    first_term = mixing(form, real_table, values_re + values_im)
    second_term = mixing(form, real_table + imag_table, values_im)
    third_term = mixing(form, imag_table - real_table, values_re)
    return (first_term - second_term, first_term + third_term)


def channel_filter(field, spectrum):
    coarse = spectrum.shape[1]
    span = spectrum.shape[2]
    count = coarse // 2
    cols = field.shape[1]
    length = coarse * span
    pencil = field.reshape(count, span, cols)
    coarse_ids = jnp.arange(coarse, dtype=jnp.int32)
    cos_a, sin_a = angle_grid(coarse_ids, jnp.arange(count, dtype=jnp.int32), coarse)
    part_re = mixing("ka,amc->kmc", cos_a, pencil)
    part_im = -mixing("ka,amc->kmc", sin_a, pencil)
    fine_ids = jnp.arange(span, dtype=jnp.int32)
    cos_t, sin_t = angle_grid(coarse_ids, fine_ids, length)
    cos_t = cos_t[:, :, None]
    sin_t = sin_t[:, :, None]
    turned_re = part_re * cos_t + part_im * sin_t
    turned_im = part_im * cos_t - part_re * sin_t
    cos_s, sin_s = angle_grid(fine_ids, fine_ids, span)
    full_re, full_im = complex_mix("qm,kmc->kqc", cos_s, -sin_s, turned_re, turned_im)
    filt_re = spectrum[0].astype(jnp.float32)
    filt_im = spectrum[1].astype(jnp.float32)
    prod_re = filt_re * full_re - filt_im * full_im
    prod_im = filt_re * full_im + filt_im * full_re
    inner_re, inner_im = complex_mix("mq,kqc->kmc", cos_s, sin_s, prod_re, prod_im)
    back_re = inner_re * cos_t - inner_im * sin_t
    back_im = inner_im * cos_t + inner_re * sin_t
    result = mixing("ka,kmc->amc", cos_a, back_re) - mixing("ka,kmc->amc", sin_a, back_im)
    return (result / length).reshape(count * span, cols)


def shards(
    signal,
    gate_first,
    gate_second,
    spectrum_first,
    spectrum_second,
    skip_first,
    skip_second,
    out_weight,
):
    seq_index = lax.axis_index("seq")
    width = signal.shape[1]
    parts_seq = lax.axis_size("seq")
    cols = width // parts_seq
    col_sig, col_first, col_second = (
        lax.all_to_all(signal, "seq", split_axis=1, concat_axis=0, tiled=True),
        lax.all_to_all(gate_first, "seq", split_axis=1, concat_axis=0, tiled=True),
        lax.all_to_all(gate_second, "seq", split_axis=1, concat_axis=0, tiled=True),
    )
    spec_one, spec_two = (
        lax.all_to_all(spectrum_first, "seq", split_axis=3, concat_axis=1, tiled=True),
        lax.all_to_all(spectrum_second, "seq", split_axis=3, concat_axis=1, tiled=True),
    )
    skip_one = lax.dynamic_slice_in_dim(skip_first, seq_index * cols, cols, 0)
    skip_two = lax.dynamic_slice_in_dim(skip_second, seq_index * cols, cols, 0)
    values = col_sig.astype(jnp.float32)
    first_conv = channel_filter(values, spec_one) + skip_one * values
    first_out = (col_first.astype(jnp.float32) * first_conv).astype(jnp.bfloat16)
    first_vals = first_out.astype(jnp.float32)
    second_conv = channel_filter(first_vals, spec_two) + skip_two * first_vals
    mixed_cols = (col_second.astype(jnp.float32) * second_conv).astype(jnp.bfloat16)
    mixed = lax.all_to_all(mixed_cols, "seq", split_axis=0, concat_axis=1, tiled=True)
    features = lax.all_gather(mixed, "mdl", axis=1, tiled=True)
    total = jnp.dot(
        features,
        lax.all_gather(out_weight, "seq", axis=0, tiled=True),
        preferred_element_type=jnp.float32,
    )
    return total.astype(jnp.bfloat16)


def solution(mesh):
    placed = (
        P(("grp", "seq"), "mdl"),
        P(("grp", "seq"), "mdl"),
        P(("grp", "seq"), "mdl"),
        P(None, "seq", None, "mdl"),
        P(None, "seq", None, "mdl"),
        P("mdl"),
        P("mdl"),
        P("seq", "mdl"),
    )
    return jax.shard_map(
        shards, mesh=mesh, in_specs=placed, out_specs=P(("grp", "seq"), "mdl"), check_vma=False
    )
```

profile of v0, /device:TPU:0, one launch (start us, length us, event | category | flops | bytes accessed | tf_op | source)
XLA Modules:
  0.0 189.6 jit_solution(12314016013267601482)
XLA Ops:
  8.6 7.4 %all-to-all-start.4 = ((bf16[128,8,128]{2,0,1:T(8,128)(2,1)}), bf16[128,8,128]{2,0,1:T(8,128)(2,1)S(1)}, u32[]{:S(2)}, u32[]{:S(2)}) async-start(bf16[128,8,128]{2,0,1:T(8,128)(2,1)} %copy.81), calls=%async_computation.4 | async-start | bytes 524288 | tf_op jit(solution)/shard_map/all_to_all | solution.py:71
  16.0 3.7 %copy.78 = bf16[2,2,128,1024]{2,1,0,3:T(2,128)(2,1)} copy(bf16[2,2,128,1024]{3,2,1,0:T(8,128)(2,1)} %param.11) | data formatting | bytes 2097152 | tf_op args[3]
  19.7 5.2 %all-to-all-done.4 = bf16[128,8,128]{2,0,1:T(8,128)(2,1)S(1)} async-done(((bf16[128,8,128]{2,0,1:T(8,128)(2,1)}), bf16[128,8,128]{2,0,1:T(8,128)(2,1)S(1)}, u32[]{:S(2)}, u32[]{:S(2)}) %all-to-all-start.4) | async-done | bytes 262176 | tf_op jit(solution)/shard_map/all_to_all | solution.py:71
  24.9 3.6 %all-to-all-start.3 = ((bf16[2,2,128,1024]{2,1,0,3:T(2,128)(2,1)}), bf16[2,2,128,1024]{2,1,0,3:T(2,128)(2,1)S(1)}, u32[]{:S(2)}, u32[]{:S(2)}) async-start(bf16[2,2,128,1024]{2,1,0,3:T(2,128)(2,1)} %copy.78), calls=%async_computation.3 | async-start | bytes 2097152 | tf_op jit(solution)/shard_map/all_to_all | solution.py:76
  30.6 2.0 %copy.73 = bf16[2,2,128,1024]{2,1,0,3:T(2,128)(2,1)} copy(bf16[2,2,128,1024]{3,2,1,0:T(8,128)(2,1)S(1)} %copy-done.1) | data formatting | bytes 2097152 | tf_op args[4]
  37.0 2.6 %fusion.179 = (f32[16,128,128]{2,0,1:T(8,128)S(1)}, f32[16,128,128]{2,0,1:T(8,128)S(1)}, f32[16,128,128]{2,0,1:T(8,128)}) fusion(f32[16,128]{0,1:T(8,128)S(1)} %copy.84, f32[16,128,128]{2,0,1:T(8,128)S(1)} %convolution_negate_fusion.1, f32[16,128]{0,1:T(8,128)S(1)} %copy.83, bf16[128,8,128]{2,0,1:T(8,128)(2,1)S(1)} %all-to-all-done.4), kind=kOutput, calls=%fused_computation.205 | convolution fusion | flops 27002624 | bytes 4472832 | tf_op jit(solution)/shard_map/ka,amc->kmc/dot_general | solution.py:16
  39.6 29.2 %all-to-all-done.3 = bf16[2,2,128,1024]{2,1,0,3:T(2,128)(2,1)S(1)} async-done(((bf16[2,2,128,1024]{2,1,0,3:T(2,128)(2,1)}), bf16[2,2,128,1024]{2,1,0,3:T(2,128)(2,1)S(1)}, u32[]{:S(2)}, u32[]{:S(2)}) %all-to-all-start.3) | async-done | bytes 1048608 | tf_op jit(solution)/shard_map/all_to_all | solution.py:76
  68.8 4.4 %all-to-all-start.1 = ((bf16[2,2,128,1024]{2,1,0,3:T(2,128)(2,1)}), bf16[2,2,128,1024]{2,1,0,3:T(2,128)(2,1)}, u32[]{:S(2)}, u32[]{:S(2)}) async-start(bf16[2,2,128,1024]{2,1,0,3:T(2,128)(2,1)} %copy.73), calls=%async_computation.1 | async-start | bytes 2097152 | tf_op jit(solution)/shard_map/all_to_all | solution.py:77
  73.3 2.1 %fusion.22 = f32[16,128,128]{2,1,0:T(8,128)S(1)} fusion(f32[16,128,128]{2,0,1:T(8,128)S(1)} %get-tuple-element.8), kind=kOutput, calls=%fused_computation.43 | convolution fusion | flops 402882560 | bytes 2097152 | tf_op jit(solution)/shard_map/qm,kmc->kqc/dot_general | solution.py:16
  75.4 2.2 %fusion.3 = f32[16,128,128]{1,2,0:T(8,128)S(1)} fusion(f32[16,128,128]{2,1,0:T(8,128)S(1)} %fusion.22, f32[16,128,128]{2,0,1:T(8,128)S(1)} %get-tuple-element.9), kind=kOutput, calls=%fused_computation.12 | convolution fusion | flops 403177472 | bytes 3145728 | tf_op jit(solution)/shard_map/qm,kmc->kqc/dot_general | solution.py:16
  77.9 2.4 %fusion.13 = (f32[16,128,128]{1,2,0:T(8,128)S(1)}, f32[16,128,128]{1,2,0:T(8,128)S(1)}) fusion(f32[16,128,128]{1,2,0:T(8,128)S(1)} %fusion.3, bf16[1,8,2,128,128]{3,4,2,1,0:T(8,128)(2,1)S(1)} %get-tuple-element.22, bf16[1,8,2,128,128]{3,4,2,1,0:T(8,128)(2,1)S(1)} %get-tuple-element.21, f32[16,128,128]{2,1,0:T(8,128)S(1)} %fusion.22, ...), kind=kOutput, calls=%fused_computation.34 | convolution fusion | flops 405274624 | bytes 6291456 | tf_op jit(solution)/shard_map/qm,kmc->kqc/dot_general | solution.py:16
  82.8 40.1 %all-to-all-done.1 = bf16[2,2,128,1024]{2,1,0,3:T(2,128)(2,1)} async-done(((bf16[2,2,128,1024]{2,1,0,3:T(2,128)(2,1)}), bf16[2,2,128,1024]{2,1,0,3:T(2,128)(2,1)}, u32[]{:S(2)}, u32[]{:S(2)}) %all-to-all-start.1) | async-done | bytes 1048608 | tf_op jit(solution)/shard_map/all_to_all | solution.py:77
  122.9 4.3 %all-to-all-start.2 = ((bf16[128,8,128]{2,0,1:T(8,128)(2,1)}), bf16[128,8,128]{2,0,1:T(8,128)(2,1)}, u32[]{:S(2)}, u32[]{:S(2)}) async-start(bf16[128,8,128]{2,0,1:T(8,128)(2,1)} %copy.76), calls=%async_computation.2 | async-start | bytes 524288 | tf_op jit(solution)/shard_map/all_to_all | solution.py:72
  127.2 2.8 %add_bitcast_fusion.1 = (f32[16,128,128]{1,2,0:T(8,128)}, f32[16,128,128]{1,2,0:T(8,128)}) fusion(f32[16,128,128]{2,1,0:T(8,128)S(1)} %convolution_add_fusion.2, f32[16,128]{1,0:T(8,128)S(1)} %get-tuple-element.23, f32[16,128]{1,0:T(8,128)S(1)} %get-tuple-element.24, f32[16,128,128]{2,1,0:T(8,128)S(1)} %fusion.26, f32[16,128,128]{1,2,0:T(8,128)S(1)} %get-tuple-element.13), kind=kOutput, calls=%fused_computation.53 | convolution fusion | flops 404733952 | bytes 5259264 | tf_op jit(solution)/shard_map/mq,kqc->kmc/dot_general | solution.py:16
  130.0 2.6 %copy.88 = f32[16,128,128]{2,0,1:T(8,128)} copy(f32[16,128,128]{1,2,0:T(8,128)} %get-tuple-element.18) | data formatting | bytes 2097152 | tf_op jit(solution)/shard_map/sub | solution.py:50
  135.8 1.9 fusion.80
  137.7 5.7 %all-to-all-start = ((bf16[128,8,128]{2,0,1:T(8,128)(2,1)}), bf16[128,8,128]{2,0,1:T(8,128)(2,1)S(1)}, u32[]{:S(2)}, u32[]{:S(2)}) async-start(bf16[128,8,128]{2,0,1:T(8,128)(2,1)} %copy.71), calls=%async_computation | async-start | bytes 524288 | tf_op jit(solution)/shard_map/all_to_all | solution.py:73
  143.4 1.9 fusion.11
  147.1 2.1 %fusion.18 = f32[16,128,128]{2,1,0:T(8,128)S(1)} fusion(f32[16,128,128]{2,0,1:T(8,128)S(1)} %get-tuple-element.5), kind=kOutput, calls=%fused_computation.39 | convolution fusion | flops 402882560 | bytes 2097152 | tf_op jit(solution)/shard_map/qm,kmc->kqc/dot_general | solution.py:16
  149.2 2.2 %fusion.1 = f32[16,128,128]{1,2,0:T(8,128)S(1)} fusion(f32[16,128,128]{2,1,0:T(8,128)S(1)} %fusion.18, f32[16,128,128]{2,0,1:T(8,128)S(1)} %get-tuple-element.6), kind=kOutput, calls=%fused_computation.5 | convolution fusion | flops 403177472 | bytes 3145728 | tf_op jit(solution)/shard_map/qm,kmc->kqc/dot_general | solution.py:16
  151.4 2.4 %fusion.15 = (f32[16,128,128]{1,2,0:T(8,128)S(1)}, f32[16,128,128]{1,2,0:T(8,128)S(1)}) fusion(f32[16,128,128]{1,2,0:T(8,128)S(1)} %fusion.1, bf16[1,8,2,128,128]{3,4,2,1,0:T(8,128)(2,1)S(1)} %get-tuple-element.20, bf16[1,8,2,128,128]{3,4,2,1,0:T(8,128)(2,1)S(1)} %get-tuple-element.19, f32[16,128,128]{2,1,0:T(8,128)S(1)} %fusion.18, ...), kind=kOutput, calls=%fused_computation.36 | convolution fusion | flops 405274624 | bytes 6291456 | tf_op jit(solution)/shard_map/qm,kmc->kqc/dot_general | solution.py:16
  162.7 14.0 %all_to_all.88 = bf16[8,128,128]{2,1,0:T(8,128)(2,1)S(1)} all-to-all(bf16[8,128,128]{2,1,0:T(8,128)(2,1)S(1)} %copy.95), channel_id=1, replica_groups=mesh['grp'=2,'seq'=8,'mdl'=2] {'seq'}, dimensions={0} | all-to-all | bytes 524288 | tf_op jit(solution)/shard_map/all_to_all | solution.py:87
  176.9 2.2 %all_gather.6 = bf16[128,2048]{0,1:T(8,128)(2,1)S(1)} all-gather(bf16[128,1024]{0,1:T(8,128)(2,1)S(1)} %bitcast.132), channel_id=1, replica_groups=mesh['grp'=2,'seq'=8,'mdl'=2] {'mdl'}, dimensions={1}, use_global_device_ids=true | all-gather | bytes 786432 | tf_op jit(solution)/shard_map/all_gather | solution.py:88
  179.1 3.6 %convolution_convert_fusion = bf16[128,1024]{1,0:T(8,128)(2,1)} fusion(bf16[128,2048]{0,1:T(8,128)(2,1)S(1)} %all_gather.6, bf16[2048,1024]{1,0:T(8,128)(2,1)} %all-gather.2.cloned.1.call-done), kind=kOutput, calls=%fused_computation.32 | convolution fusion | flops 537001984 | bytes 4980736 | tf_op jit(solution)/shard_map/dot_general | solution.py:89
  (45 shorter events, 25.3 us)
Async XLA Ops:
  6.5 23.0 %copy-start.2 = (bf16[128,1024]{1,0:T(8,128)(2,1)S(1)}, bf16[128,1024]{1,0:T(8,128)(2,1)}, u32[]{:S(2)}) copy-start(bf16[128,1024]{1,0:T(8,128)(2,1)} %param.9) | copy-start | bytes 786436
  6.5 24.0 %copy-start.1 = (bf16[2,2,128,1024]{3,2,1,0:T(8,128)(2,1)S(1)}, bf16[2,2,128,1024]{3,2,1,0:T(8,128)(2,1)}, u32[]{:S(2)}) copy-start(bf16[2,2,128,1024]{3,2,1,0:T(8,128)(2,1)} %param.12) | copy-start | bytes 3145732
  8.6 26.7 %copy-start.3 = (bf16[128,1024]{1,0:T(8,128)(2,1)S(1)}, bf16[128,1024]{1,0:T(8,128)(2,1)}, u32[]{:S(2)}) copy-start(bf16[128,1024]{1,0:T(8,128)(2,1)} %param.10) | copy-start | bytes 786436
  8.6 16.3 %all-to-all-start.4 = ((bf16[128,8,128]{2,0,1:T(8,128)(2,1)}), bf16[128,8,128]{2,0,1:T(8,128)(2,1)S(1)}, u32[]{:S(2)}, u32[]{:S(2)}) async-start(bf16[128,8,128]{2,0,1:T(8,128)(2,1)} %copy.81), calls=%async_computation.4 | async-start | bytes 524288 | tf_op jit(solution)/shard_map/all_to_all | solution.py:71
  24.9 43.9 %all-to-all-start.3 = ((bf16[2,2,128,1024]{2,1,0,3:T(2,128)(2,1)}), bf16[2,2,128,1024]{2,1,0,3:T(2,128)(2,1)S(1)}, u32[]{:S(2)}, u32[]{:S(2)}) async-start(bf16[2,2,128,1024]{2,1,0,3:T(2,128)(2,1)} %copy.78), calls=%async_computation.3 | async-start | bytes 2097152 | tf_op jit(solution)/shard_map/all_to_all | solution.py:76
  28.5 150.6 %all-gather.2.cloned.1.call-start = ((), (), s32[]{:S(2)}) async-start(), calls=%async_computation.6 | async-start | bytes 4718592 | tf_op jit(solution)/shard_map/all_gather | solution.py:91
  68.8 54.1 %all-to-all-start.1 = ((bf16[2,2,128,1024]{2,1,0,3:T(2,128)(2,1)}), bf16[2,2,128,1024]{2,1,0,3:T(2,128)(2,1)}, u32[]{:S(2)}, u32[]{:S(2)}) async-start(bf16[2,2,128,1024]{2,1,0,3:T(2,128)(2,1)} %copy.73), calls=%async_computation.1 | async-start | bytes 2097152 | tf_op jit(solution)/shard_map/all_to_all | solution.py:77
  75.4 2.5 %copy-start = (f32[16,128,128]{2,0,1:T(8,128)S(1)}, f32[16,128,128]{2,0,1:T(8,128)}, u32[]{:S(2)}) copy-start(f32[16,128,128]{2,0,1:T(8,128)} %get-tuple-element.10) | copy-start | bytes 3145732
  122.9 14.7 %all-to-all-start.2 = ((bf16[128,8,128]{2,0,1:T(8,128)(2,1)}), bf16[128,8,128]{2,0,1:T(8,128)(2,1)}, u32[]{:S(2)}, u32[]{:S(2)}) async-start(bf16[128,8,128]{2,0,1:T(8,128)(2,1)} %copy.76), calls=%async_computation.2 | async-start | bytes 524288 | tf_op jit(solution)/shard_map/all_to_all | solution.py:72
  137.7 24.2 %all-to-all-start = ((bf16[128,8,128]{2,0,1:T(8,128)(2,1)}), bf16[128,8,128]{2,0,1:T(8,128)(2,1)S(1)}, u32[]{:S(2)}, u32[]{:S(2)}) async-start(bf16[128,8,128]{2,0,1:T(8,128)(2,1)} %copy.71), calls=%async_computation | async-start | bytes 524288 | tf_op jit(solution)/shard_map/all_to_all | solution.py:73
  158.0 3.8 %copy-start.4 = (f32[128]{0:T(128)S(1)}, f32[128]{0:T(128)}, u32[]{:S(2)}) copy-start(f32[128]{0:T(128)} %dynamic_slice.7) | copy-start | bytes 1540
Sparse Core Ops, SparseCore 0:
  31.5 104.5 all-gather.1
where the time goes:
time: 191 us; the launch traced here: 190 us
  waiting for transfers between devices  75.3 us (39%)
  matrix products  37.8 us (20%)
  starting transfers between devices  25.4 us (13%)
  local copies, waits for them, and re-layouts  21.1 us (11%)
  blocking collectives  16.2 us (8%)
  between operations  13.7 us (7%)
    all_to_all x1, waiting for transfers between devices, shards(): lax.all_to_all(spectrum_second, 'seq', split_axis=3, concat_axis=1, tiled...  40.1 us
    dot_general x20, matrix products, mixing(): return jnp.einsum(form, left, right, precision=lax.Precision.HIGHEST)  34.2 us
    all_to_all x1, waiting for transfers between devices, shards(): lax.all_to_all(spectrum_first, 'seq', split_axis=3, concat_axis=1, tiled=...  29.2 us
    all_to_all x1, blocking collectives, shards(): lax.all_to_all(mixed_cols, 'seq', split_axis=0, concat_axis=1, tiled=True)  14 us
    all_to_all x1, starting transfers between devices, shards(): lax.all_to_all(signal, 'seq', split_axis=1, concat_axis=0, tiled=True)  7.38 us
    unnamed x15, local copies, waits for them, and re-layouts  7.3 us
    all_to_all x1, starting transfers between devices, shards(): lax.all_to_all(gate_second, 'seq', split_axis=1, concat_axis=0, tiled=True)  5.69 us
    all_to_all x1, waiting for transfers between devices, shards(): lax.all_to_all(signal, 'seq', split_axis=1, concat_axis=0, tiled=True)  5.23 us
  transfers between devices with their start and end apart: 6, of which 3 were waited for; matrix products, arithmetic and copies ran while one was open for 28% of the time, Pallas kernels for 0%

commit v1 on v0

--- a/solution.py
+++ b/solution.py
@@ -1,9 +1,16 @@
+import functools
 import math
 
 import jax
 import jax.numpy as jnp
+import numpy as np
 from jax import lax
+from jax.experimental import pallas as pl
+from jax.experimental.pallas import tpu as pltpu
 from jax.sharding import PartitionSpec as P
+
+MESH = pl.DeviceIdType.MESH
+LANES = 128
 
 
 def angle_grid(first, second, modulus):
@@ -53,7 +60,7 @@
     return (result / length).reshape(count * span, cols)
 
 
-def shards(
+def plain_shards(
     signal,
     gate_first,
     gate_second,
@@ -94,6 +101,378 @@
     return total.astype(jnp.bfloat16)
 
 
+def turn_tables(span, coarse):
+    ids = np.arange(span)
+    fine = 2.0 * math.pi * (ids[:, None] * ids[None, :] % span) / span
+    step = 2.0 * math.pi * np.broadcast_to(ids[:, None], (span, span)) / (span * coarse)
+    return np.stack(
+        [np.cos(fine), np.sin(fine), np.cos(step), np.sin(step), np.cos(step).T, np.sin(step).T]
+    ).astype(np.float32)
+
+
+def weighted(terms):
+    total = None
+    for weight, value in terms:
+        if abs(weight) < 1e-12:
+            continue
+        if abs(weight - 1.0) < 1e-12:
+            term = value
+        elif abs(weight + 1.0) < 1e-12:
+            total = -value if total is None else total - value
+            continue
+        else:
+            term = value * weight
+        total = term if total is None else total + term
+    return total
+
+
+def coarse_forward(field, parts, rows):
+    count, span, cols = field.shape
+    half = count // 2
+
+    @pl.loop(0, span // rows)
+    def _(i):
+        at = pl.multiple_of(i * rows, rows)
+        f = [field[a, pl.ds(at, rows), :].astype(jnp.float32) for a in range(count)]
+        plus = {a: f[a] + f[count - a] for a in range(1, half)}
+        minus = {a: f[a] - f[count - a] for a in range(1, half)}
+        for j in range(count + 1):
+            for_cos, for_sin = (plus, minus) if j % 2 == 0 else (minus, plus)
+            angle = [math.pi * a * j / count for a in range(count)]
+            real = weighted(
+                [(1.0, f[0]), (math.cos(angle[half]), f[half])]
+                + [(math.cos(angle[a]), for_cos[a]) for a in range(1, half)]
+            )
+            imag = weighted(
+                [(-math.sin(angle[half]), f[half])]
+                + [(-math.sin(angle[a]), for_sin[a]) for a in range(1, half)]
+            )
+            if imag is None:
+                imag = jnp.zeros_like(real)
+            parts[j, pl.ds(at, rows), :] = real.astype(jnp.bfloat16)
+            parts[j, pl.ds(pl.multiple_of(span + at, rows), rows), :] = imag.astype(jnp.bfloat16)
+
+
+def fine_stage(parts, spectrum, there, back_table, back, k, count, span):
+    @pl.loop(0, count)
+    def _(b):
+        j = 2 * b + k
+        source = jnp.where(j <= count, j, 2 * count - j)
+        full = jnp.dot(there[j], parts[source], preferred_element_type=jnp.float32)
+        full_re, full_im = full[:span], full[span:]
+        filt_re = spectrum[k, b, 0].astype(jnp.float32)
+        filt_im = spectrum[k, b, 1].astype(jnp.float32)
+        prod_re = filt_re * full_re - filt_im * full_im
+        prod_im = filt_re * full_im + filt_im * full_re
+        prod = jnp.concatenate([prod_re.astype(jnp.bfloat16), prod_im.astype(jnp.bfloat16)], axis=0)
+        back[j] = jnp.dot(back_table[j], prod, preferred_element_type=jnp.float32)
+
+
+def coarse_back(back, field, gate, skip, result, rows):
+    count, span, cols = field.shape
+    half = count // 2
+    direct = jnp.broadcast_to(skip, (rows, cols))
+
+    @pl.loop(0, span // rows)
+    def _(i):
+        at = pl.multiple_of(i * rows, rows)
+        low = pl.multiple_of(span + at, rows)
+
+        def real(j):
+            return back[j, pl.ds(at, rows), :]
+
+        def imag(j):
+            return back[j, pl.ds(low, rows), :]
+
+        re = [real(0)] + [real(j) + real(2 * count - j) for j in range(1, count)] + [real(count)]
+        im = [None] + [imag(j) - imag(2 * count - j) for j in range(1, count)] + [None]
+        even_re = [re[j] + re[count - j] for j in range(half)]
+        odd_re = [re[j] - re[count - j] for j in range(half)]
+        even_im = [None] + [im[j] - im[count - j] for j in range(1, half)]
+        odd_im = [None] + [im[j] + im[count - j] for j in range(1, half)]
+        for a in range(count):
+            use_re, use_im = (even_re, even_im) if a % 2 == 0 else (odd_re, odd_im)
+            angle = [math.pi * a * j / count for j in range(half + 1)]
+            total = weighted(
+                [(math.cos(angle[j]), use_re[j]) for j in range(half)]
+                + [(math.cos(angle[half]), re[half]), (-math.sin(angle[half]), im[half])]
+                + [(-math.sin(angle[j]), use_im[j]) for j in range(1, half)]
+            )
+            values = field[a, pl.ds(at, rows), :].astype(jnp.float32)
+            total = total + direct * values
+            gated = gate[a, pl.ds(at, rows), :].astype(jnp.float32) * total
+            result[a, pl.ds(at, rows), :] = gated.astype(jnp.bfloat16)
+
+
+def build_tables(tab, there, back_table, turn, count, span):
+    turn[0] = tab[0]
+    turn[1] = tab[1]
+    turn[2] = tab[0]
+    turn[3] = tab[1]
+    scale = 1.0 / (2 * count * span)
+
+    @pl.loop(0, 2 * count)
+    def _(j):
+        flip = jnp.where(j > count, -1.0, 1.0).astype(jnp.float32)
+        cos_a, sin_a, cos_b, sin_b = turn[0], turn[1], turn[2], turn[3]
+        there[j, :span, :span] = cos_a.astype(jnp.bfloat16)
+        there[j, :span, span:] = (sin_a * flip).astype(jnp.bfloat16)
+        there[j, span:, :span] = (-sin_a).astype(jnp.bfloat16)
+        there[j, span:, span:] = (cos_a * flip).astype(jnp.bfloat16)
+        cos_s, sin_s = cos_b * scale, sin_b * scale
+        back_table[j, :span, :span] = cos_s.astype(jnp.bfloat16)
+        back_table[j, :span, span:] = (-sin_s).astype(jnp.bfloat16)
+        back_table[j, span:, :span] = sin_s.astype(jnp.bfloat16)
+        back_table[j, span:, span:] = cos_s.astype(jnp.bfloat16)
+        turn[0] = cos_a * tab[4] - sin_a * tab[5]
+        turn[1] = sin_a * tab[4] + cos_a * tab[5]
+        turn[2] = cos_b * tab[2] - sin_b * tab[3]
+        turn[3] = sin_b * tab[2] + cos_b * tab[3]
+
+
+def block_kernel(
+    count,
+    signal,
+    gate_one,
+    gate_two,
+    spec_one,
+    spec_two,
+    skip_one,
+    skip_two,
+    tab,
+    out,
+    in_signal,
+    in_gate_one,
+    in_gate_two,
+    in_spec_one,
+    in_spec_two,
+    in_skip,
+    there,
+    back_table,
+    turn,
+    parts,
+    back,
+    second_field,
+    mixed,
+    send_sem,
+    own_sem,
+    recv_sem,
+):
+    g, s, m = lax.axis_index("grp"), lax.axis_index("seq"), lax.axis_index("mdl")
+    span, cols = in_signal.shape[1], in_signal.shape[2]
+    total = 4 * count
+    me = (g * count + s) * 2 + m
+
+    barrier = pltpu.get_barrier_semaphore()
+
+    @pl.loop(1, total)
+    def _(o):
+        peer = lax.rem(me + o, total)
+        pl.semaphore_signal(
+            barrier,
+            inc=1,
+            device_id=(peer // (2 * count), lax.rem(peer // 2, count), lax.rem(peer, 2)),
+            device_id_type=MESH,
+        )
+
+    pl.semaphore_wait(barrier, total - 1)
+
+    def columns(block):
+        return pl.ds(pl.multiple_of(block * cols, cols), cols)
+
+    def remote(source, target, slot, own, where):
+        return pltpu.make_async_remote_copy(
+            src_ref=source,
+            dst_ref=target,
+            send_sem=own_sem.at[slot] if own else send_sem.at[slot],
+            recv_sem=recv_sem.at[slot],
+            device_id=where,
+            device_id_type=MESH,
+        )
+
+    def local(source, target, slot):
+        return pltpu.make_async_copy(source, target, recv_sem.at[slot])
+
+    def swap(source, target, slot):
+        @pl.when(g == m)
+        def _():
+            local(source, target, slot).start()
+
+        @pl.when(g != m)
+        def _():
+            remote(source, target, slot, True, (m, s, g)).start()
+
+    def send_rows(array, buffer, slot):
+        @pl.loop(1, count)
+        def _(o):
+            c = lax.rem(s + o, count)
+            remote(array.at[:, columns(c)], buffer.at[s], slot, False, (m, c, g)).start()
+
+        swap(array.at[:, columns(s)], buffer.at[s], slot)
+
+    def send_spectrum(array, buffer, slot):
+        @pl.when(g == m)
+        def _():
+            @pl.loop(1, count)
+            def _(o):
+                c = lax.rem(s + o, count)
+                for k in range(2):
+                    remote(
+                        array.at[:, k, :, columns(c)], buffer.at[k, s], slot, False, (g, c, k)
+                    ).start()
+
+            remote(
+                array.at[:, 1 - m, :, columns(s)], buffer.at[1 - m, s], slot, True, (g, s, 1 - m)
+            ).start()
+            local(array.at[:, m, :, columns(s)], buffer.at[m, s], slot).start()
+
+    def relay(buffer, slot):
+        return remote(buffer.at[m], buffer.at[m], slot, False, (g, s, 1 - m))
+
+    def take(view, slot):
+        pltpu.make_async_copy(view, view, recv_sem.at[slot]).wait()
+
+    send_rows(signal, in_signal, 0)
+    send_spectrum(spec_one, in_spec_one, 3)
+    send_rows(gate_one, in_gate_one, 1)
+    swap(skip_one, in_skip.at[0], 7)
+    swap(skip_two, in_skip.at[1], 8)
+    send_spectrum(spec_two, in_spec_two, 5)
+    send_rows(gate_two, in_gate_two, 2)
+
+    build_tables(tab, there, back_table, turn, count, span)
+
+    take(in_signal, 0)
+    coarse_forward(in_signal, parts, 16)
+    take(in_spec_one.at[m], 3)
+    relay(in_spec_one, 4).start()
+    fine_stage(parts, in_spec_one, there, back_table, back, m, count, span)
+    take(in_spec_one.at[1 - m], 4)
+    fine_stage(parts, in_spec_one, there, back_table, back, 1 - m, count, span)
+    take(in_gate_one, 1)
+    take(in_skip.at[0], 7)
+    take(in_skip.at[1], 8)
+    coarse_back(back, in_signal, in_gate_one, in_skip[0, pl.ds(s, 1), :], second_field, 16)
+    coarse_forward(second_field, parts, 16)
+    take(in_spec_two.at[m], 5)
+    relay(in_spec_two, 6).start()
+    fine_stage(parts, in_spec_two, there, back_table, back, m, count, span)
+    take(in_spec_two.at[1 - m], 6)
+    fine_stage(parts, in_spec_two, there, back_table, back, 1 - m, count, span)
+    take(in_gate_two, 2)
+    coarse_back(back, second_field, in_gate_two, in_skip[1, pl.ds(s, 1), :], mixed, 16)
+
+    width = count * cols
+    mine = columns(g * count + s)
+
+    @pl.loop(1, count)
+    def _(o):
+        c = lax.rem(s + o, count)
+        remote(mixed.at[c], out.at[:, mine], 9, False, (m, c, g)).start()
+
+    swap(mixed.at[s], out.at[:, mine], 9)
+    half = out.at[:, pl.ds(pl.multiple_of(m * width, width), width)]
+    other = out.at[:, pl.ds(pl.multiple_of((1 - m) * width, width), width)]
+    take(half, 9)
+    final = remote(half, half, 10, False, (g, s, 1 - m))
+    final.start()
+    take(other, 10)
+
+    def sent(view, slot, own=False):
+        pltpu.make_async_copy(view, view, own_sem.at[slot] if own else send_sem.at[slot]).wait()
+
+    final.wait_send()
+    relay(in_spec_one, 4).wait_send()
+    relay(in_spec_two, 6).wait_send()
+    most = pl.ds(0, count - 1)
+    for slot in (0, 1, 2, 9):
+        sent(in_signal.at[most], slot)
+
+    @pl.when(g != m)
+    def _():
+        for slot in (0, 1, 2, 9):
+            sent(in_signal.at[0], slot, True)
+        sent(in_skip.at[0], 7, True)
+        sent(in_skip.at[1], 8, True)
+
+    @pl.when(g == m)
+    def _():
+        for slot in (3, 5):
+            sent(in_spec_one.at[:, most], slot)
+            sent(in_spec_one.at[0, 0], slot, True)
+
+
+def direct_shards(
+    signal,
+    gate_first,
+    gate_second,
+    spectrum_first,
+    spectrum_second,
+    skip_first,
+    skip_second,
+    out_weight,
+):
+    count = lax.axis_size("seq")
+    span, width = signal.shape
+    cols = width // count
+    coarse = 2 * count
+    weight = lax.all_gather(out_weight, "seq", axis=0, tiled=True)
+    anywhere = pl.BlockSpec(memory_space=pl.ANY)
+    vmem = pl.BlockSpec(memory_space=pltpu.VMEM)
+    bf16, f32 = jnp.bfloat16, jnp.float32
+    features = pl.pallas_call(
+        functools.partial(block_kernel, count),
+        out_shape=jax.ShapeDtypeStruct((span, 2 * width), bf16),
+        in_specs=[anywhere] * 7 + [vmem],
+        out_specs=vmem,
+        scratch_shapes=[
+            pltpu.VMEM((count, span, cols), bf16),
+            pltpu.VMEM((count, span, cols), bf16),
+            pltpu.VMEM((count, span, cols), bf16),
+            pltpu.VMEM((2, count, 2, span, cols), bf16),
+            pltpu.VMEM((2, count, 2, span, cols), bf16),
+            pltpu.VMEM((2, count, cols), f32),
+            pltpu.VMEM((coarse, 2 * span, 2 * span), bf16),
+            pltpu.VMEM((coarse, 2 * span, 2 * span), bf16),
+            pltpu.VMEM((4, span, span), f32),
+            pltpu.VMEM((count + 1, 2 * span, cols), bf16),
+            pltpu.VMEM((coarse, 2 * span, cols), f32),
+            pltpu.VMEM((count, span, cols), bf16),
+            pltpu.VMEM((count, span, cols), bf16),
+            pltpu.SemaphoreType.DMA((11,)),
+            pltpu.SemaphoreType.DMA((11,)),
+            pltpu.SemaphoreType.DMA((11,)),
+        ],
+        compiler_params=pltpu.CompilerParams(
+            collective_id=0, has_side_effects=True, vmem_limit_bytes=32 * 1024 * 1024
+        ),
+        cost_estimate=pl.CostEstimate(
+            flops=16 * coarse * span * span * cols, bytes_accessed=1 << 26, transcendentals=0
+        ),
+    )(
+        signal,
+        gate_first,
+        gate_second,
+        spectrum_first,
+        spectrum_second,
+        skip_first.reshape(count, cols),
+        skip_second.reshape(count, cols),
+        jnp.asarray(turn_tables(span, coarse)),
+    )
+    total = jnp.dot(features, weight, preferred_element_type=jnp.float32)
+    return total.astype(jnp.bfloat16)
+
+
+def shards(*arrays):
+    count = lax.axis_size("seq")
+    span, width = arrays[0].shape
+    pairs = lax.axis_size("grp") == 2 and lax.axis_size("mdl") == 2
+    whole_tiles = width == count * LANES and span == LANES and count % 8 == 0 and count <= 16
+    if pairs and whole_tiles and arrays[3].shape[1] == 2:
+        return direct_shards(*arrays)
+    return plain_shards(*arrays)
+
+
 def solution(mesh):
     placed = (
         P(("grp", "seq"), "mdl"),

time: 191 us -> 134 us (0.70)
  Pallas kernels: 0 us -> 108 us
  waiting for transfers between devices: 75.3 us -> 0.73 us
  matrix products: 37.8 us -> 3.61 us
  starting transfers between devices: 25.4 us -> 0.01 us
  blocking collectives: 16.2 us -> 0 us
  local copies, waits for them, and re-layouts: 21.1 us -> 7.66 us
    pallas_call x0 -> x1, Pallas kernels: none -> 108 us  [direct_shards(): pl.pallas_call(functools.partial(block_kernel, count), out_shape=jax.Shap...]
    all_to_all x5 -> x0, waiting for transfers between devices: 74.6 us -> none  [the longest x1 40.1 us: shards(): lax.all_to_all(spectrum_second, 'seq', split_axis=3, concat_axis=1, tiled...]
    dot_general x21 -> x1, matrix products: 37.8 us -> 3.61 us  [direct_shards(): total = jnp.dot(features, weight, preferred_element_type=jnp.float32)]
    all_to_all x5 -> x0, starting transfers between devices: 25.4 us -> none  [the longest x1 7.38 us: shards(): lax.all_to_all(signal, 'seq', split_axis=1, concat_axis=0, tiled=True)]
    all_to_all x1 -> x0, blocking collectives: 14 us -> none  [shards(): lax.all_to_all(mixed_cols, 'seq', split_axis=0, concat_axis=1, tiled=True)]
    all_to_all x6 -> x0, local copies, waits for them, and re-layouts: 4.46 us -> none  [the longest x1 1.46 us: shards(): lax.all_to_all(spectrum_second, 'seq', split_axis=3, concat_axis=1, tiled...]
    sub x2 -> x0, local copies, waits for them, and re-layouts: 4.02 us -> none  [channel_filter(): back_re = inner_re * cos_t - inner_im * sin_t]
    dynamic_slice x2 -> x0, local copies, waits for them, and re-layouts: 2.68 us -> none  [the longest x1 1.35 us: shards(): skip_two = lax.dynamic_slice_in_dim(skip_second, seq_index * cols, cols, 0)]
  transfers between devices with their start and end apart: 6 -> 1, of which waited for: 3 -> 0; matrix products, arithmetic and copies ran while one was open for 28% -> 0% of each run, Pallas kernels for 0% -> 81%
where the time goes in v1:
time: 134 us
  Pallas kernels  108 us (81%)
  between operations  13.4 us (10%)
  local copies, waits for them, and re-layouts  7.66 us (6%)
  matrix products  3.61 us (3%)
    pallas_call x1, Pallas kernels, direct_shards(): pl.pallas_call(functools.partial(block_kernel, count), out_shape=jax.Shap...  108 us
    unnamed x16, local copies, waits for them, and re-layouts  7.66 us
    dot_general x1, matrix products, direct_shards(): total = jnp.dot(features, weight, preferred_element_type=jnp.float32)  3.61 us
  transfers between devices with their start and end apart: 1, of which 0 were waited for; matrix products, arithmetic and copies ran while one was open for 0% of the time, Pallas kernels for 81%

profile of v1, /device:TPU:0, one launch (start us, length us, event | category | flops | bytes accessed | tf_op | source)
XLA Modules:
  0.0 133.5 jit_solution(7983130357882694367)
XLA Ops:
  6.5 0.0 all-gather.2.cloned.1.call-start
  6.5 0.7 all-gather.2.cloned.1.call-update
  7.3 0.0 copy-start
  7.3 1.2 copy-done
  8.5 0.0 copy-start.1
  8.5 1.2 copy-done.1
  9.7 0.0 copy-start.2
  9.7 1.0 copy-done.2
  10.7 0.0 copy-start.3
  10.7 0.9 copy-done.3
  11.7 0.0 copy-start.4
  11.7 0.9 copy-done.4
  12.6 0.0 copy-start.5
  12.6 0.9 copy-done.5
  13.6 0.0 copy-start.6
  13.6 0.7 copy-done.6
  14.2 0.0 copy-start.7
  14.2 0.7 copy-done.7
  14.9 108.1 %shard_map.91 = bf16[128,2048]{1,0:T(8,128)(2,1)S(1)} custom-call(bf16[128,1024]{1,0:T(8,128)(2,1)S(1)} %copy-done.3, bf16[128,1024]{1,0:T(8,128)(2,1)S(1)} %copy-done.4, bf16[128,1024]{1,0:T(8,128)(2,1)S(1)} %copy-done.5, bf16[2,2,128,1024]{3,2,1,0:T(8,128)(2,1)S(1)} %copy-done, bf16[2,2,128,1024]{3,2,1,0:T(8,128)(2,1)S(1)} %copy-done.1, ...), custom_call_target="tpu_custom_call" | custom-call | flops 536870912 | bytes 67108864 | tf_op jit(solution)/shard_map/pallas_call | solution.py:423
  123.0 0.0 all-gather.2.cloned.1.call-done
  123.1 3.6 %convolution_convert_fusion = bf16[128,1024]{1,0:T(8,128)(2,1)} fusion(bf16[128,2048]{1,0:T(8,128)(2,1)S(1)} %shard_map.91, bf16[2048,1024]{1,0:T(8,128)(2,1)} %all-gather.2.cloned.1.call-done), kind=kOutput, calls=%fused_computation | convolution fusion | flops 537001984 | bytes 4980736 | tf_op jit(solution)/shard_map/dot_general | solution.py:462
Async XLA Ops:
  6.5 116.5 %all-gather.2.cloned.1.call-start = ((), (), s32[]{:S(2)}) async-start(), calls=%async_computation | async-start | bytes 4718592 | tf_op jit(solution)/shard_map/all_gather | solution.py:419
  7.3 1.2 copy-start
  8.5 1.2 copy-start.1
  9.7 1.0 copy-start.2
  10.7 0.9 copy-start.3
  11.7 0.9 copy-start.4
  12.6 0.9 copy-start.5
  13.6 0.7 copy-start.6
  14.2 0.7 copy-start.7
Sparse Core Ops, SparseCore 0:
  9.5 108.3 all-gather.1

commit v2 on v1

--- a/solution.py
+++ b/solution.py
@@ -149,8 +149,18 @@
             )
             if imag is None:
                 imag = jnp.zeros_like(real)
-            parts[j, pl.ds(at, rows), :] = real.astype(jnp.bfloat16)
-            parts[j, pl.ds(pl.multiple_of(span + at, rows), rows), :] = imag.astype(jnp.bfloat16)
+            for top, value in ((at, real), (pl.multiple_of(span + at, rows), imag)):
+                high = value.astype(jnp.bfloat16)
+                parts[j, pl.ds(top, rows), :cols] = high
+                parts[j, pl.ds(top, rows), cols:] = (value - high.astype(jnp.float32)).astype(
+                    jnp.bfloat16
+                )
+
+
+def split_dot(table, j, both, cols):
+    main = jnp.dot(table[j, 0], both, preferred_element_type=jnp.float32)
+    rest = jnp.dot(table[j, 1], both[:, :cols], preferred_element_type=jnp.float32)
+    return main[:, :cols] + (main[:, cols:] + rest)
 
 
 def fine_stage(parts, spectrum, there, back_table, back, k, count, span):
@@ -158,14 +168,17 @@
     def _(b):
         j = 2 * b + k
         source = jnp.where(j <= count, j, 2 * count - j)
-        full = jnp.dot(there[j], parts[source], preferred_element_type=jnp.float32)
+        full = split_dot(there, j, parts[source], back.shape[2])
         full_re, full_im = full[:span], full[span:]
         filt_re = spectrum[k, b, 0].astype(jnp.float32)
         filt_im = spectrum[k, b, 1].astype(jnp.float32)
         prod_re = filt_re * full_re - filt_im * full_im
         prod_im = filt_re * full_im + filt_im * full_re
-        prod = jnp.concatenate([prod_re.astype(jnp.bfloat16), prod_im.astype(jnp.bfloat16)], axis=0)
-        back[j] = jnp.dot(back_table[j], prod, preferred_element_type=jnp.float32)
+        prod = jnp.concatenate([prod_re, prod_im], axis=0)
+        high = prod.astype(jnp.bfloat16)
+        low = (prod - high.astype(jnp.float32)).astype(jnp.bfloat16)
+        both = jnp.concatenate([high, low], axis=1)
+        back[j] = split_dot(back_table, j, both, back.shape[2])
 
 
 def coarse_back(back, field, gate, skip, result, rows):
@@ -215,15 +228,18 @@
     def _(j):
         flip = jnp.where(j > count, -1.0, 1.0).astype(jnp.float32)
         cos_a, sin_a, cos_b, sin_b = turn[0], turn[1], turn[2], turn[3]
-        there[j, :span, :span] = cos_a.astype(jnp.bfloat16)
-        there[j, :span, span:] = (sin_a * flip).astype(jnp.bfloat16)
-        there[j, span:, :span] = (-sin_a).astype(jnp.bfloat16)
-        there[j, span:, span:] = (cos_a * flip).astype(jnp.bfloat16)
         cos_s, sin_s = cos_b * scale, sin_b * scale
-        back_table[j, :span, :span] = cos_s.astype(jnp.bfloat16)
-        back_table[j, :span, span:] = (-sin_s).astype(jnp.bfloat16)
-        back_table[j, span:, :span] = sin_s.astype(jnp.bfloat16)
-        back_table[j, span:, span:] = cos_s.astype(jnp.bfloat16)
+        entries = (
+            (there, cos_a, sin_a * flip, -sin_a, cos_a * flip),
+            (back_table, cos_s, -sin_s, sin_s, cos_s),
+        )
+        places = ((0, 0), (0, 1), (1, 0), (1, 1))
+        for table, *blocks in entries:
+            for (row, col), value in zip(places, blocks):
+                at = (slice(row * span, row * span + span), slice(col * span, col * span + span))
+                high = value.astype(jnp.bfloat16)
+                table[(j, 0) + at] = high
+                table[(j, 1) + at] = (value - high.astype(jnp.float32)).astype(jnp.bfloat16)
         turn[0] = cos_a * tab[4] - sin_a * tab[5]
         turn[1] = sin_a * tab[4] + cos_a * tab[5]
         turn[2] = cos_b * tab[2] - sin_b * tab[3]
@@ -239,6 +255,7 @@
     spec_two,
     skip_one,
     skip_two,
+    weight,
     tab,
     out,
     in_signal,
@@ -254,9 +271,19 @@
     back,
     second_field,
     mixed,
+    features,
+    totals,
+    rows_all,
     send_sem,
     own_sem,
     recv_sem,
+    line_send,
+    line_recv,
+    side_send,
+    side_recv,
+    plane_send,
+    plane_recv,
+    own_copy,
 ):
     g, s, m = lax.axis_index("grp"), lax.axis_index("seq"), lax.axis_index("mdl")
     span, cols = in_signal.shape[1], in_signal.shape[2]
@@ -332,27 +359,160 @@
     def take(view, slot):
         pltpu.make_async_copy(view, view, recv_sem.at[slot]).wait()
 
+    levels = count // 2
+    z, x = s // 2, lax.rem(s, 2)
+    beside = s + 1 - 2 * x
+    depth = weight.shape[0]
+    piece = depth // 2
+
+    def chunk(block, half):
+        return rows_all.at[pl.ds(pl.multiple_of(block * depth + half * piece, piece), piece), :]
+
+    def post(block, source, sems, where):
+        return pltpu.make_async_remote_copy(
+            src_ref=source,
+            dst_ref=chunk(block, g),
+            send_sem=sems[0],
+            recv_sem=sems[1],
+            device_id=where,
+            device_id_type=MESH,
+        )
+
+    def along(block, source, way):
+        level = block // 2
+        step = 2 if way == 0 else -2
+        return post(
+            block, source, (line_send.at[way, level], line_recv.at[level]), (g, s + step, m)
+        )
+
+    def across(block, source):
+        level = block // 2
+        return post(block, source, (side_send.at[level], side_recv.at[level]), (g, beside, m))
+
+    def over(block):
+        return post(
+            block, chunk(block, g), (plane_send.at[block], plane_recv.at[block]), (1 - g, s, m)
+        )
+
+    def landed(block, half, sem):
+        view = chunk(block, half)
+        pltpu.make_async_copy(view, view, sem).wait()
+
+    own_rows = pltpu.make_async_copy(
+        weight, rows_all.at[pl.ds(pl.multiple_of(s * depth, depth), depth), :], own_copy.at[0]
+    )
+    own_piece = weight.at[pl.ds(pl.multiple_of(g * piece, piece), piece), :]
+
+    def weight_step(distance):
+        if distance == 0:
+            own_rows.start()
+
+            @pl.when(z < levels - 1)
+            def _():
+                along(s, own_piece, 0).start()
+
+            @pl.when(z > 0)
+            def _():
+                along(s, own_piece, 1).start()
+
+            across(s, own_piece).start()
+            return
+
+        @pl.when(z >= distance)
+        def _():
+            block = s - 2 * distance
+            landed(block, g, line_recv.at[z - distance])
+
+            @pl.when(z < levels - 1)
+            def _():
+                along(block, chunk(block, g), 0).start()
+
+            across(block, chunk(block, g)).start()
+            over(block).start()
+
+        @pl.when(z + distance < levels)
+        def _():
+            block = s + 2 * distance
+            landed(block, g, line_recv.at[z + distance])
+
+            @pl.when(z > 0)
+            def _():
+                along(block, chunk(block, g), 1).start()
+
+            across(block, chunk(block, g)).start()
+            over(block).start()
+
+    def weight_side(distance):
+        @pl.when(z >= distance)
+        def _():
+            block = beside - 2 * distance
+            landed(block, g, side_recv.at[z - distance])
+            over(block).start()
+
+        if distance > 0:
+
+            @pl.when(z + distance < levels)
+            def _():
+                block = beside + 2 * distance
+                landed(block, g, side_recv.at[z + distance])
+                over(block).start()
+
+    def weight_end():
+        own_rows.wait()
+
+        @pl.loop(1, count)
+        def _(o):
+            block = lax.rem(s + o, count)
+            landed(block, 1 - g, plane_recv.at[block])
+
+    def weight_sent():
+        for distance in range(levels):
+
+            @pl.when((z >= distance) & (z < levels - 1))
+            def _():
+                along(s - 2 * distance, chunk(0, g), 0).wait_send()
+
+            @pl.when((z + distance < levels) & (z > 0))
+            def _():
+                along(s + 2 * distance, chunk(0, g), 1).wait_send()
+
+        @pl.loop(0, levels)
+        def _(level):
+            across(2 * level + x, chunk(0, g)).wait_send()
+
+        @pl.loop(1, count)
+        def _(o):
+            over(lax.rem(s + o, count)).wait_send()
+
     send_rows(signal, in_signal, 0)
+    weight_step(0)
     send_spectrum(spec_one, in_spec_one, 3)
     send_rows(gate_one, in_gate_one, 1)
     swap(skip_one, in_skip.at[0], 7)
     swap(skip_two, in_skip.at[1], 8)
+
+    build_tables(tab, there, back_table, turn, count, span)
+
+    weight_step(1)
+    weight_side(0)
     send_spectrum(spec_two, in_spec_two, 5)
     send_rows(gate_two, in_gate_two, 2)
-
-    build_tables(tab, there, back_table, turn, count, span)
-
     take(in_signal, 0)
     coarse_forward(in_signal, parts, 16)
+    weight_step(2)
+    weight_side(1)
     take(in_spec_one.at[m], 3)
     relay(in_spec_one, 4).start()
     fine_stage(parts, in_spec_one, there, back_table, back, m, count, span)
+    weight_step(3)
+    weight_side(2)
     take(in_spec_one.at[1 - m], 4)
     fine_stage(parts, in_spec_one, there, back_table, back, 1 - m, count, span)
     take(in_gate_one, 1)
     take(in_skip.at[0], 7)
     take(in_skip.at[1], 8)
     coarse_back(back, in_signal, in_gate_one, in_skip[0, pl.ds(s, 1), :], second_field, 16)
+    weight_side(3)
     coarse_forward(second_field, parts, 16)
     take(in_spec_two.at[m], 5)
     relay(in_spec_two, 6).start()
@@ -368,15 +528,41 @@
     @pl.loop(1, count)
     def _(o):
         c = lax.rem(s + o, count)
-        remote(mixed.at[c], out.at[:, mine], 9, False, (m, c, g)).start()
-
-    swap(mixed.at[s], out.at[:, mine], 9)
-    half = out.at[:, pl.ds(pl.multiple_of(m * width, width), width)]
-    other = out.at[:, pl.ds(pl.multiple_of((1 - m) * width, width), width)]
+        remote(mixed.at[c], features.at[:, mine], 9, False, (m, c, g)).start()
+
+    swap(mixed.at[s], features.at[:, mine], 9)
+    weight_end()
+    first = pl.multiple_of(m * width, width)
+    second = pl.multiple_of((1 - m) * width, width)
+    half = features.at[:, pl.ds(first, width)]
+    other = features.at[:, pl.ds(second, width)]
     take(half, 9)
     final = remote(half, half, 10, False, (g, s, 1 - m))
     final.start()
+    tile = 2 * cols
+
+    @pl.loop(0, width // tile)
+    def _(i):
+        at = pl.ds(pl.multiple_of(i * tile, tile), tile)
+        totals[:, at] = jnp.dot(
+            features[:, pl.ds(first, width)],
+            rows_all[pl.ds(first, width), at],
+            preferred_element_type=jnp.float32,
+        )
+
     take(other, 10)
+
+    @pl.loop(0, width // tile)
+    def _(i):
+        at = pl.ds(pl.multiple_of(i * tile, tile), tile)
+        more = jnp.dot(
+            features[:, pl.ds(second, width)],
+            rows_all[pl.ds(second, width), at],
+            preferred_element_type=jnp.float32,
+        )
+        out[:, at] = (totals[:, at] + more).astype(out.dtype)
+
+    weight_sent()
 
     def sent(view, slot, own=False):
         pltpu.make_async_copy(view, view, own_sem.at[slot] if own else send_sem.at[slot]).wait()
@@ -416,14 +602,13 @@
     span, width = signal.shape
     cols = width // count
     coarse = 2 * count
-    weight = lax.all_gather(out_weight, "seq", axis=0, tiled=True)
-    anywhere = pl.BlockSpec(memory_space=pl.ANY)
+    anywhere = pl.BlockSpec(memory_space=pltpu.HBM)
     vmem = pl.BlockSpec(memory_space=pltpu.VMEM)
     bf16, f32 = jnp.bfloat16, jnp.float32
-    features = pl.pallas_call(
+    return pl.pallas_call(
         functools.partial(block_kernel, count),
-        out_shape=jax.ShapeDtypeStruct((span, 2 * width), bf16),
-        in_specs=[anywhere] * 7 + [vmem],
+        out_shape=jax.ShapeDtypeStruct((span, width), bf16),
+        in_specs=[anywhere] * 8 + [vmem],
         out_specs=vmem,
         scratch_shapes=[
             pltpu.VMEM((count, span, cols), bf16),
@@ -432,19 +617,29 @@
             pltpu.VMEM((2, count, 2, span, cols), bf16),
             pltpu.VMEM((2, count, 2, span, cols), bf16),
             pltpu.VMEM((2, count, cols), f32),
-            pltpu.VMEM((coarse, 2 * span, 2 * span), bf16),
-            pltpu.VMEM((coarse, 2 * span, 2 * span), bf16),
+            pltpu.VMEM((coarse, 2, 2 * span, 2 * span), bf16),
+            pltpu.VMEM((coarse, 2, 2 * span, 2 * span), bf16),
             pltpu.VMEM((4, span, span), f32),
-            pltpu.VMEM((count + 1, 2 * span, cols), bf16),
+            pltpu.VMEM((count + 1, 2 * span, 2 * cols), bf16),
             pltpu.VMEM((coarse, 2 * span, cols), f32),
             pltpu.VMEM((count, span, cols), bf16),
             pltpu.VMEM((count, span, cols), bf16),
+            pltpu.VMEM((span, 2 * width), bf16),
+            pltpu.VMEM((span, width), f32),
+            pltpu.VMEM((2 * width, width), bf16),
             pltpu.SemaphoreType.DMA((11,)),
             pltpu.SemaphoreType.DMA((11,)),
             pltpu.SemaphoreType.DMA((11,)),
+            pltpu.SemaphoreType.DMA((2, count // 2)),
+            pltpu.SemaphoreType.DMA((count // 2,)),
+            pltpu.SemaphoreType.DMA((count // 2,)),
+            pltpu.SemaphoreType.DMA((count // 2,)),
+            pltpu.SemaphoreType.DMA((count,)),
+            pltpu.SemaphoreType.DMA((count,)),
+            pltpu.SemaphoreType.DMA((1,)),
         ],
         compiler_params=pltpu.CompilerParams(
-            collective_id=0, has_side_effects=True, vmem_limit_bytes=32 * 1024 * 1024
+            collective_id=0, has_side_effects=True, vmem_limit_bytes=62 * 1024 * 1024
         ),
         cost_estimate=pl.CostEstimate(
             flops=16 * coarse * span * span * cols, bytes_accessed=1 << 26, transcendentals=0
@@ -457,17 +652,16 @@
         spectrum_second,
         skip_first.reshape(count, cols),
         skip_second.reshape(count, cols),
+        out_weight,
         jnp.asarray(turn_tables(span, coarse)),
     )
-    total = jnp.dot(features, weight, preferred_element_type=jnp.float32)
-    return total.astype(jnp.bfloat16)
 
 
 def shards(*arrays):
     count = lax.axis_size("seq")
     span, width = arrays[0].shape
     pairs = lax.axis_size("grp") == 2 and lax.axis_size("mdl") == 2
-    whole_tiles = width == count * LANES and span == LANES and count % 8 == 0 and count <= 16
+    whole_tiles = width == count * LANES and span == LANES and count == 8
     if pairs and whole_tiles and arrays[3].shape[1] == 2:
         return direct_shards(*arrays)
     return plain_shards(*arrays)

time: 134 us -> 85.2 us (0.64)
  Pallas kernels: 108 us -> 83.3 us
  between operations: 13.4 us -> 0.01 us
  local copies, waits for them, and re-layouts: 7.66 us -> 1.67 us
  matrix products: 3.61 us -> 0 us
    pallas_call x1, Pallas kernels: 108 us -> 83.3 us  [direct_shards(): pl.pallas_call(functools.partial(block_kernel, count), out_shape=jax.Shap...]
    unnamed x16 -> x1, local copies, waits for them, and re-layouts: 7.66 us -> 1.67 us
    dot_general x1 -> x0, matrix products: 3.61 us -> none  [direct_shards(): total = jnp.dot(features, weight, preferred_element_type=jnp.float32)]
  transfers between devices with their start and end apart: 1 -> 0, of which waited for: 0 -> 0; matrix products, arithmetic and copies ran while one was open for 0% -> 0% of each run, Pallas kernels for 81% -> 0%
where the time goes in v2:
time: 85.2 us; the launch traced here: 85 us
  Pallas kernels  83.3 us (98%)
  local copies, waits for them, and re-layouts  1.67 us (2%)
    pallas_call x1, Pallas kernels, direct_shards(): pl.pallas_call(functools.partial(block_kernel, count), out_shape=jax.Shap...  83.3 us

profile of v2, /device:TPU:0, one launch (start us, length us, event | category | flops | bytes accessed | tf_op | source)
XLA Modules:
  0.0 85.0 jit_solution(6428655396056735503)
XLA Ops:
  0.0 83.3 %shard_map.91 = bf16[128,1024]{1,0:T(8,128)(2,1)} custom-call(bf16[128,1024]{1,0:T(8,128)(2,1)} %signal.1, bf16[128,1024]{1,0:T(8,128)(2,1)} %gate_one.1, bf16[128,1024]{1,0:T(8,128)(2,1)} %gate_two.1, bf16[2,2,128,1024]{3,2,1,0:T(8,128)(2,1)} %spec_one.1, bf16[2,2,128,1024]{3,2,1,0:T(8,128)(2,1)} %spec_two.1, f32[8,128]{1,0:T(8,128)} %bitcast.2, ...), custom_call_target="tpu_custom_call" | custom-call | flops 536870912 | bytes 67108864 | tf_op jit(solution)/shard_map/pallas_call | solution.py:608
  83.3 1.7 %copy.11 = bf16[128,1024]{1,0:T(8,128)(2,1)} copy(bf16[128,1024]{1,0:T(8,128)(2,1)} %shard_map.91) | data formatting | bytes 524288

commit v3 on v2

--- a/solution.py
+++ b/solution.py
@@ -164,7 +164,7 @@
 
 
 def fine_stage(parts, spectrum, there, back_table, back, k, count, span):
-    @pl.loop(0, count)
+    @pl.loop(0, count, unroll=4)
     def _(b):
         j = 2 * b + k
         source = jnp.where(j <= count, j, 2 * count - j)
@@ -284,6 +284,8 @@
     plane_send,
     plane_recv,
     own_copy,
+    mix_recv,
+    pass_send,
 ):
     g, s, m = lax.axis_index("grp"), lax.axis_index("seq"), lax.axis_index("mdl")
     span, cols = in_signal.shape[1], in_signal.shape[2]
@@ -495,27 +497,27 @@
 
     weight_step(1)
     weight_side(0)
-    send_spectrum(spec_two, in_spec_two, 5)
-    send_rows(gate_two, in_gate_two, 2)
     take(in_signal, 0)
     coarse_forward(in_signal, parts, 16)
     weight_step(2)
     weight_side(1)
+    send_rows(gate_two, in_gate_two, 2)
+    send_spectrum(spec_two, in_spec_two, 5)
     take(in_spec_one.at[m], 3)
     relay(in_spec_one, 4).start()
     fine_stage(parts, in_spec_one, there, back_table, back, m, count, span)
-    weight_step(3)
-    weight_side(2)
     take(in_spec_one.at[1 - m], 4)
     fine_stage(parts, in_spec_one, there, back_table, back, 1 - m, count, span)
     take(in_gate_one, 1)
     take(in_skip.at[0], 7)
     take(in_skip.at[1], 8)
+    weight_step(3)
+    weight_side(2)
     coarse_back(back, in_signal, in_gate_one, in_skip[0, pl.ds(s, 1), :], second_field, 16)
-    weight_side(3)
     coarse_forward(second_field, parts, 16)
     take(in_spec_two.at[m], 5)
     relay(in_spec_two, 6).start()
+    weight_side(3)
     fine_stage(parts, in_spec_two, there, back_table, back, m, count, span)
     take(in_spec_two.at[1 - m], 6)
     fine_stage(parts, in_spec_two, there, back_table, back, 1 - m, count, span)
@@ -525,20 +527,51 @@
     width = count * cols
     mine = columns(g * count + s)
 
+    def deliver(block, own=False):
+        return pltpu.make_async_remote_copy(
+            src_ref=mixed.at[block],
+            dst_ref=features.at[:, mine],
+            send_sem=own_sem.at[9] if own else send_sem.at[9],
+            recv_sem=mix_recv.at[s],
+            device_id=(m, block, g),
+            device_id_type=MESH,
+        )
+
+    def pass_on(block):
+        view = features.at[:, columns(m * count + block)]
+        return pltpu.make_async_remote_copy(
+            src_ref=view,
+            dst_ref=view,
+            send_sem=pass_send.at[block],
+            recv_sem=recv_sem.at[10],
+            device_id=(g, s, 1 - m),
+            device_id_type=MESH,
+        )
+
+    @pl.when(g == m)
+    def _():
+        pltpu.make_async_copy(mixed.at[s], features.at[:, mine], mix_recv.at[s]).start()
+
+    @pl.when(g != m)
+    def _():
+        deliver(s, True).start()
+
     @pl.loop(1, count)
     def _(o):
-        c = lax.rem(s + o, count)
-        remote(mixed.at[c], features.at[:, mine], 9, False, (m, c, g)).start()
-
-    swap(mixed.at[s], features.at[:, mine], 9)
+        deliver(lax.rem(s + o, count)).start()
+
     weight_end()
     first = pl.multiple_of(m * width, width)
     second = pl.multiple_of((1 - m) * width, width)
-    half = features.at[:, pl.ds(first, width)]
     other = features.at[:, pl.ds(second, width)]
-    take(half, 9)
-    final = remote(half, half, 10, False, (g, s, 1 - m))
-    final.start()
+
+    @pl.loop(0, count)
+    def _(o):
+        block = lax.rem(s + count - o, count)
+        view = features.at[:, columns(m * count + block)]
+        pltpu.make_async_copy(view, view, mix_recv.at[block]).wait()
+        pass_on(block).start()
+
     tile = 2 * cols
 
     @pl.loop(0, width // tile)
@@ -567,7 +600,11 @@
     def sent(view, slot, own=False):
         pltpu.make_async_copy(view, view, own_sem.at[slot] if own else send_sem.at[slot]).wait()
 
-    final.wait_send()
+
+    @pl.loop(0, count)
+    def _(block):
+        pass_on(block).wait_send()
+
     relay(in_spec_one, 4).wait_send()
     relay(in_spec_two, 6).wait_send()
     most = pl.ds(0, count - 1)
@@ -637,6 +674,8 @@
             pltpu.SemaphoreType.DMA((count,)),
             pltpu.SemaphoreType.DMA((count,)),
             pltpu.SemaphoreType.DMA((1,)),
+            pltpu.SemaphoreType.DMA((count,)),
+            pltpu.SemaphoreType.DMA((count,)),
         ],
         compiler_params=pltpu.CompilerParams(
             collective_id=0, has_side_effects=True, vmem_limit_bytes=62 * 1024 * 1024

time: 85.2 us -> 81.5 us (0.957)
  Pallas kernels: 83.3 us -> 79.7 us
    pallas_call x1, Pallas kernels: 83.3 us -> 79.7 us  [direct_shards(): pl.pallas_call(functools.partial(block_kernel, count), out_shape=jax.Shap...]
where the time goes in v3:
time: 81.5 us; the launch traced here: 81.3 us
  Pallas kernels  79.7 us (98%)
  local copies, waits for them, and re-layouts  1.67 us (2%)
    pallas_call x1, Pallas kernels, direct_shards(): pl.pallas_call(functools.partial(block_kernel, count), out_shape=jax.Shap...  79.7 us
    unnamed x1, local copies, waits for them, and re-layouts  1.67 us

profile of v3, /device:TPU:0, one launch (start us, length us, event | category | flops | bytes accessed | tf_op | source)
XLA Modules:
  0.0 81.3 jit_solution(1262492697826263387)
XLA Ops:
  0.0 79.7 %shard_map.91 = bf16[128,1024]{1,0:T(8,128)(2,1)} custom-call(bf16[128,1024]{1,0:T(8,128)(2,1)} %signal.1, bf16[128,1024]{1,0:T(8,128)(2,1)} %gate_one.1, bf16[128,1024]{1,0:T(8,128)(2,1)} %gate_two.1, bf16[2,2,128,1024]{3,2,1,0:T(8,128)(2,1)} %spec_one.1, bf16[2,2,128,1024]{3,2,1,0:T(8,128)(2,1)} %spec_two.1, f32[8,128]{1,0:T(8,128)} %bitcast.2, ...), custom_call_target="tpu_custom_call" | custom-call | flops 536870912 | bytes 67108864 | tf_op jit(solution)/shard_map/pallas_call | solution.py:645
  79.7 1.7 %copy.11 = bf16[128,1024]{1,0:T(8,128)(2,1)} copy(bf16[128,1024]{1,0:T(8,128)(2,1)} %shard_map.91) | data formatting | bytes 524288
